TPU v7x, 256 devices: a whole 4x4x8 slice. The times are simulated.
256 devices in a mesh: dp: 2 (over core), row: 16 (over y, x), col: 8 (over z).
Axes of the slice: x: 4, y: 4, z: 8, core: 2. Of those that a mesh axis runs over, the one named last changes fastest.
Arguments:
- features: bfloat16 [2, 256, 128, 1024], P('dp', None, 'row', 'col'), may hold values from -41 to 41, as said below
- group_kernel: bfloat16 [256, 72], replicated, may hold values from -0.75 to 0.75
- norm_gain: float32 [256], replicated, may hold values from 0.1 to 1.9
- norm_bias: float32 [256], replicated, may hold values from -3 to 3
- mix_weight: bfloat16 [256, 256], replicated, may hold values from -0.375 to 0.375
- cotangent: bfloat16 [2, 256, 128, 1024], P('dp', None, 'row', 'col'), may hold values from -6 to 6
Outputs:
- mixed: bfloat16 [2, 256, 128, 1024], P('dp', None, 'row', 'col')
- grad_features: bfloat16 [2, 256, 128, 1024], P('dp', None, 'row', 'col')
- grad_mix: float32 [256, 256], replicated
- grad_gain: float32 [256], replicated
- grad_bias: float32 [256], replicated
- grad_kernel: float32 [256, 72], replicated
- grad_whiten: float32 [2, 256, 256], P('dp')
Inputs may be any that keep to these rules, and one draw needn't show every extreme that they name: `features`: feature maps whose scale varies over channels and over cells.
All inputs are finite; a program needn't handle non-finite values.
Results may differ from a plain program's by a relative error of at most 0.0085.
Values may be sent and summed in bfloat16 or wider, within the bound.
A program may use at most 64 MiB of HBM per device.

v0:
```python
import jax
import jax.numpy as jnp
from jax import lax
from jax.sharding import PartitionSpec as P

GROUPS = 32
NEWTON = 5
EPS = 1e-05


def with_halo(block, sides, width):
    for axis, dim in sides:
        count = lax.axis_size(axis)
        forward = [(i, i + 1) for i in range(count - 1)]
        backward = [(target, source) for source, target in forward]
        low = lax.ppermute(
            lax.slice_in_dim(block, block.shape[dim] - width, None, axis=dim), axis, forward
        )
        high = lax.ppermute(lax.slice_in_dim(block, 0, width, axis=dim), axis, backward)
        block = jnp.concatenate([low, block, high], axis=dim)
    return block


def group_conv(padded, kernel):
    chans, prow, pcol = padded.shape
    height = prow - 2
    width = pcol - 2
    gwidth = chans // GROUPS
    pieces = padded.reshape(GROUPS, gwidth, prow, pcol)
    weights = kernel.reshape(GROUPS, gwidth, gwidth, 9)
    total = jnp.zeros((GROUPS, gwidth, height, width), jnp.float32)
    for position in range(9):
        shift_row, shift_col = divmod(position, 3)
        window = pieces[:, :, shift_row : shift_row + height, shift_col : shift_col + width]
        total = total + jnp.einsum(
            "goi,girw->gorw", weights[..., position], window, preferred_element_type=jnp.float32
        )
    return total.reshape(chans, height, width)


def conv_transpose(grad_pad, kernel):
    chans, prow, pcol = grad_pad.shape
    height = prow - 2
    width = pcol - 2
    gwidth = chans // GROUPS
    pieces = grad_pad.reshape(GROUPS, gwidth, prow, pcol)
    weights = kernel.reshape(GROUPS, gwidth, gwidth, 9)
    total = jnp.zeros((GROUPS, gwidth, height, width), jnp.float32)
    for position in range(9):
        shift_row, shift_col = divmod(position, 3)
        window = pieces[
            :, :, 2 - shift_row : 2 - shift_row + height, 2 - shift_col : 2 - shift_col + width
        ]
        total = total + jnp.einsum(
            "goi,gorw->girw", weights[..., position], window, preferred_element_type=jnp.float32
        )
    return total.reshape(chans, height, width)


def kernel_grad(grad_conv, padded):
    chans, height, width = grad_conv.shape
    gwidth = chans // GROUPS
    grads = grad_conv.reshape(GROUPS, gwidth, height, width)
    pieces = padded.reshape(GROUPS, gwidth, height + 2, width + 2)
    parts = []
    for position in range(9):
        shift_row, shift_col = divmod(position, 3)
        window = pieces[:, :, shift_row : shift_row + height, shift_col : shift_col + width]
        parts.append(
            jnp.einsum("gorw,girw->goi", grads, window, preferred_element_type=jnp.float32)
        )
    return jnp.stack(parts, axis=-1).reshape(chans, gwidth * 9)


def whitening(covariance):
    trace_value = jnp.trace(covariance)
    normed = covariance / trace_value
    proj = jnp.eye(covariance.shape[0], dtype=jnp.float32)
    for step in range(NEWTON):
        cube = jnp.dot(
            jnp.dot(proj, proj, precision=lax.Precision.HIGHEST),
            proj,
            precision=lax.Precision.HIGHEST,
        )
        proj = 0.5 * (3.0 * proj - jnp.dot(cube, normed, precision=lax.Precision.HIGHEST))
    return proj / jnp.sqrt(trace_value)


def local(features, group_kernel, norm_gain, norm_bias, mix_weight, cotangent):
    image = features[0]
    chans, height, width = image.shape
    local_cells = height * width
    cells = height * lax.axis_size("row") * width * lax.axis_size("col")
    scenes = features.shape[0] * lax.axis_size("dp")
    eye_mat = jnp.eye(chans, dtype=jnp.float32)
    padded = with_halo(image, (("row", 1), ("col", 2)), 1)
    conv = group_conv(padded, group_kernel).astype(jnp.bfloat16)
    flat = conv.reshape(chans, local_cells)
    channel_mean = lax.psum(jnp.sum(flat, axis=1, dtype=jnp.float32), ("row", "col")) / cells
    centered = flat.astype(jnp.float32) - channel_mean[:, None]
    moments = jnp.dot(centered, centered.T, precision=lax.Precision.HIGHEST)
    covariance = lax.psum(moments, ("row", "col")) / cells + EPS * eye_mat
    whiten = whitening(covariance)
    normed = jnp.dot(whiten, centered, precision=lax.Precision.HIGHEST)
    shifted = norm_gain[:, None] * normed + norm_bias[:, None]
    gate = jax.nn.sigmoid(shifted)
    act = (shifted * gate).astype(jnp.bfloat16)
    mixed = (
        image.reshape(chans, local_cells).astype(jnp.float32)
        + jnp.dot(mix_weight, act, preferred_element_type=jnp.float32)
    ).astype(jnp.bfloat16)
    upstream = cotangent[0].reshape(chans, local_cells)
    dact = jnp.dot(mix_weight.T, upstream, preferred_element_type=jnp.float32)
    dshift = dact * gate * (1.0 + shifted * (1.0 - gate))
    mix_part = jnp.dot(upstream, act.T, preferred_element_type=jnp.float32)
    gain_part = jnp.sum(dshift * normed, axis=1)
    bias_part = jnp.sum(dshift, axis=1)
    dnormed = (norm_gain[:, None] * dshift).astype(jnp.bfloat16)
    white_part = jnp.dot(dnormed, flat.T, preferred_element_type=jnp.float32)
    sum_part = jnp.sum(dnormed, axis=1, dtype=jnp.float32)
    white_total, grad_sum = lax.psum((white_part, sum_part), ("row", "col"))
    dwhiten = white_total - jnp.outer(grad_sum, channel_mean)
    white_out = (dwhiten / jnp.sqrt(jnp.float32(cells)))[None]
    unused, pullback = jax.vjp(whitening, covariance)
    dcov = pullback(dwhiten)[0]
    dsym = 0.5 * (dcov + dcov.T)
    left_side = jnp.concatenate([whiten.T, dsym * (2.0 / cells)], axis=1)
    right_side = jnp.concatenate(
        [dnormed.astype(jnp.float32) - (grad_sum / cells)[:, None], centered], axis=0
    )
    dconv = jnp.dot(left_side, right_side, precision=lax.Precision.HIGHEST).astype(jnp.bfloat16)
    dconv = dconv.reshape(chans, height, width)
    grad_pad = with_halo(dconv, (("row", 1), ("col", 2)), 1)
    grad_image = (cotangent[0].astype(jnp.float32) + conv_transpose(grad_pad, group_kernel)).astype(
        jnp.bfloat16
    )
    kernel_part = kernel_grad(dconv, padded)
    scale = 1.0 / jnp.sqrt(jnp.float32(scenes * cells))
    grad_mix, grad_gain, grad_bias, grad_kernel = lax.psum(
        (mix_part, gain_part, bias_part, kernel_part), ("dp", "row", "col")
    )
    return (
        mixed.reshape(features.shape),
        grad_image.reshape(features.shape),
        grad_mix * scale,
        grad_gain * scale,
        grad_bias * scale,
        grad_kernel * scale,
        white_out,
    )


def solution(mesh):
    in_specs = (P("dp", None, "row", "col"), P(), P(), P(), P(), P("dp", None, "row", "col"))
    out_specs = (
        P("dp", None, "row", "col"),
        P("dp", None, "row", "col"),
        P(),
        P(),
        P(),
        P(),
        P("dp", None, None),
    )
    return jax.shard_map(local, mesh=mesh, in_specs=in_specs, out_specs=out_specs, check_vma=False)
```

profile of v0, /device:TPU:1, one launch (start us, length us, event | category | flops | bytes accessed | tf_op | source)
XLA Modules:
  0.0 1363.5 jit_solution(14939398661312466481)
XLA Ops:
  8.4 3.9 collective-permute-start
  15.0 2.3 collective-permute-done.1
  18.1 3.5 collective-permute-start.2
  32.4 296.3 %psum.56 = f32[256]{0:T(256)S(1)} all-reduce(f32[256]{0:T(256)S(1)} %reduce_sum.72), channel_id=1, replica_groups=mesh['dp'=2,'row'=16,'col'=8] {'row','col'}, use_global_device_ids=true, to_apply=%region_1.0 | all-reduce | flops 256 | bytes 2048 | tf_op jit(solution)/shard_map/psum | solution.py:99
  328.7 1.9 fusion.24
  331.4 258.6 %all-reduce.6.cloned.1.call-done = f32[256,256]{1,0:T(8,128)} async-done(((f32[256,256]{1,0:T(8,128)}), f32[256,256]{1,0:T(8,128)}) %all-reduce.6.cloned.1.call-update) | async-done | bytes 262160 | tf_op jit(solution)/shard_map/psum | solution.py:102
  599.1 1.7 fusion.217
  603.6 1.7 fusion.216
  608.2 2.9 fusion.79
  613.5 2.1 fusion.220
  617.5 291.8 %psum.59 = f32[256]{0:T(256)S(1)} all-reduce(f32[256]{0:T(256)S(1)} %get-tuple-element.62), channel_id=1, replica_groups=mesh['dp'=2,'row'=16,'col'=8] {'row','col'}, use_global_device_ids=true, to_apply=%region_6.7 | all-reduce | flops 256 | bytes 2048 | tf_op jit(solution)/shard_map/psum | solution.py:121
  909.5 2.3 convolution_bitcast_fusion.1
  912.9 2.1 copy.273
  915.0 131.0 %all-reduce = (f32[256]{0:T(256)S(1)}, f32[256]{0:T(256)S(1)}) all-reduce(f32[256]{0:T(256)} %get-tuple-element.36, f32[256]{0:T(256)S(1)} %get-tuple-element.35), channel_id=1, replica_groups=mesh['dp'=2,'row'=16,'col'=8] {'dp','row','col'}, use_global_device_ids=true, to_apply=%region_11.12 | all-reduce | flops 512 | bytes 4096 | tf_op jit(solution)/shard_map/psum | solution.py:139
  1047.8 2.3 fusion.90
  1064.4 1.6 convolution_add_fusion.18
  1069.4 1.8 multiply_reduce_fusion.1
  1072.1 2.9 fusion.8
  1079.0 3.2 collective-permute-start.4
  1084.1 3.6 collective-permute-done.5
  1088.3 3.7 collective-permute-start.6
  1092.4 1.5 collective-permute-start.7
  1095.0 2.9 copy.272
  1111.4 241.7 %all-reduce.10.cloned.1.call-done = (f32[256,256]{0,1:T(8,128)}, f32[256,72]{1,0:T(8,128)}) async-done(((f32[256,256]{0,1:T(8,128)}, f32[256,72]{1,0:T(8,128)}), (f32[256,256]{0,1:T(8,128)}, f32[256,72]{1,0:T(8,128)})) %all-reduce.10.cloned.1.call-update) | async-done | bytes 335888 | tf_op jit(solution)/shard_map/psum | solution.py:139
  (303 shorter events, 77.3 us)
Async XLA Ops:
  7.2 606.3 %copy-start = (bf16[256,256]{1,0:T(8,128)(2,1)S(1)}, bf16[256,256]{1,0:T(8,128)(2,1)}, u32[]{:S(2)}) copy-start(bf16[256,256]{1,0:T(8,128)(2,1)} %param.10) | copy-start | bytes 393220
  7.2 6.7 copy-start.76
  7.2 582.8 %all-reduce.6.cloned.1.call-start = ((), (), s32[]{:S(2)}) async-start(), calls=%async_computation | async-start | bytes 524288 | tf_op jit(solution)/shard_map/psum | solution.py:102
  8.4 6.6 collective-permute-start
  12.3 5.0 collective-permute-start.1
  15.0 578.5 %copy-start.51 = (f32[256,256]{1,0:T(8,128)}, f32[256,256]{1,0:T(8,128)S(1)}, u32[]{:S(2)}) copy-start(f32[256,256]{1,0:T(8,128)S(1)} %fusion.88) | copy-start | bytes 786436
  17.7 5.6 copy-start.20
  18.1 8.2 collective-permute-start.2
  22.0 4.7 collective-permute-start.3
  25.5 5.1 copy-start.63
  25.7 5.3 copy-start.61
  25.8 5.4 copy-start.59
  26.0 5.6 copy-start.57
  26.1 5.8 copy-start.55
  330.7 717.2 %all-reduce.8.cloned.1.call-start = ((), (), s32[]{:S(2)}) async-start(), calls=%async_computation.1 | async-start | bytes 524288 | tf_op jit(solution)/shard_map/psum | solution.py:121
  590.9 17.2 %copy-start.3 = (f32[256,256]{1,0:T(8,128)}, f32[256,256]{1,0:T(8,128)S(1)}, u32[]{:S(2)}) copy-start(f32[256,256]{1,0:T(8,128)S(1)} %multiply_add_fusion.1) | copy-start | bytes 786436
  617.4 294.3 %copy-start.2 = (f32[1,256,8,128]{1,3,2,0:T(8,128)S(1)}, f32[1,256,8,128]{1,3,2,0:T(8,128)}, u32[]{:S(2)}) copy-start(f32[1,256,8,128]{1,3,2,0:T(8,128)} %copy.199) | copy-start | bytes 3145732
  617.5 735.6 %all-reduce.10.cloned.1.call-start = ((), (), s32[]{:S(2)}) async-start(), calls=%async_computation.2 | async-start | bytes 786432 | tf_op jit(solution)/shard_map/psum | solution.py:139
  1079.0 4.9 collective-permute-start.4
  1082.6 5.0 collective-permute-start.5
  1087.9 6.0 copy-start.23
  1088.3 11.3 collective-permute-start.6
  1092.4 7.7 collective-permute-start.7
  1109.7 246.9 %copy-start.1 = (bf16[256,256]{1,0:T(8,128)(2,1)S(1)}, bf16[256,256]{1,0:T(8,128)(2,1)}, u32[]{:S(2)}) copy-start(bf16[256,256]{1,0:T(8,128)(2,1)} %param.10) | copy-start | bytes 393220
  (66 other events, 125.1 us)
Sparse Core Ops, SparseCore 0:
  330.8 259.1 all-reduce.5
  617.6 213.4 all-reduce.7
  1099.8 253.2 all-reduce.9
where the time goes:
time: 1370 us; the launch traced here: 1360 us
  blocking collectives  719 us (52%)
  waiting for transfers between devices  506 us (37%)
  matrix products  55.7 us (4%)
  local copies, waits for them, and re-layouts  33.5 us (2%)
  starting transfers between devices  20.5 us (1%)
  between operations  19 us (1%)
    psum x1, blocking collectives, local(): lax.psum(jnp.sum(flat, axis=1, dtype=jnp.float32), ('row', 'col')) / cells  296 us
    psum x1, blocking collectives, local(): white_total, grad_sum = lax.psum((white_part, sum_part), ('row', 'col'))  292 us
    psum x1, waiting for transfers between devices, local(): covariance = lax.psum(moments, ('row', 'col')) / cells + EPS * eye_mat  259 us
    psum x1, waiting for transfers between devices, local(): lax.psum((mix_part, gain_part, bias_part, kernel_part), ('dp', 'row', 'co...  242 us
    psum x1, blocking collectives, local(): lax.psum((mix_part, gain_part, bias_part, kernel_part), ('dp', 'row', 'co...  131 us
  transfers between devices with their start and end apart: 11, of which 4 were waited for; matrix products, arithmetic and copies ran while one was open for 2% of the time, Pallas kernels for 0%

commit v1 on v0

--- a/solution.py
+++ b/solution.py
@@ -6,6 +6,11 @@
 GROUPS = 32
 NEWTON = 5
 EPS = 1e-05
+
+
+def by_each_axis(x, axis_one, axis_two):
+    partial = lax.psum(x, axis_one)
+    return lax.psum(partial, axis_two)
 
 
 def with_halo(block, sides, width):
@@ -99,7 +104,7 @@
     channel_mean = lax.psum(jnp.sum(flat, axis=1, dtype=jnp.float32), ("row", "col")) / cells
     centered = flat.astype(jnp.float32) - channel_mean[:, None]
     moments = jnp.dot(centered, centered.T, precision=lax.Precision.HIGHEST)
-    covariance = lax.psum(moments, ("row", "col")) / cells + EPS * eye_mat
+    covariance = by_each_axis(moments, "col", "row") / cells + EPS * eye_mat
     whiten = whitening(covariance)
     normed = jnp.dot(whiten, centered, precision=lax.Precision.HIGHEST)
     shifted = norm_gain[:, None] * normed + norm_bias[:, None]

time: 1370 us -> 1320 us (0.964)
  waiting for transfers between devices: 506 us -> 462 us
    psum x1 -> x2, waiting for transfers between devices: 259 us -> 213 us  [the longest x1 114 us: by_each_axis(): partial = lax.psum(x, axis_one)]
  transfers between devices with their start and end apart: 11 -> 12, of which waited for: 4 -> 6; matrix products, arithmetic and copies ran while one was open for 2% -> 2% of each run, Pallas kernels for 0% -> 0%
where the time goes in v1:
time: 1320 us
  blocking collectives  716 us (54%)
  waiting for transfers between devices  462 us (35%)
  matrix products  53.5 us (4%)
  local copies, waits for them, and re-layouts  34.9 us (3%)
  starting transfers between devices  20.5 us (2%)
  between operations  19 us (1%)
    psum x1, blocking collectives, local(): lax.psum(jnp.sum(flat, axis=1, dtype=jnp.float32), ('row', 'col')) / cells  295 us
    psum x1, blocking collectives, local(): white_total, grad_sum = lax.psum((white_part, sum_part), ('row', 'col'))  293 us
    psum x1, waiting for transfers between devices, local(): lax.psum((mix_part, gain_part, bias_part, kernel_part), ('dp', 'row', 'co...  242 us
    psum x1, blocking collectives, local(): lax.psum((mix_part, gain_part, bias_part, kernel_part), ('dp', 'row', 'co...  128 us
    psum x1, waiting for transfers between devices, by_each_axis(): partial = lax.psum(x, axis_one)  114 us
    psum x1, waiting for transfers between devices, by_each_axis(): return lax.psum(partial, axis_two)  99.1 us
  transfers between devices with their start and end apart: 12, of which 6 were waited for; matrix products, arithmetic and copies ran while one was open for 2% of the time, Pallas kernels for 0%

profile of v1, /device:TPU:1, one launch (start us, length us, event | category | flops | bytes accessed | tf_op | source)
XLA Modules:
  0.0 1316.3 jit_solution(576588908860825181)
XLA Ops:
  8.4 3.9 collective-permute-start
  14.4 2.9 collective-permute-done.1
  18.1 3.5 collective-permute-start.2
  32.3 294.8 %psum.63 = f32[256]{0:T(256)S(1)} all-reduce(f32[256]{0:T(256)S(1)} %reduce_sum.72), channel_id=1, replica_groups=mesh['dp'=2,'row'=16,'col'=8] {'row','col'}, use_global_device_ids=true, to_apply=%region_1.0 | all-reduce | flops 256 | bytes 2048 | tf_op jit(solution)/shard_map/psum | solution.py:104
  327.2 1.9 fusion.24
  331.3 113.5 %all-reduce.7.cloned.1.call-done = f32[256,256]{1,0:T(8,128)} async-done(((f32[256,256]{1,0:T(8,128)}), f32[256,256]{1,0:T(8,128)}) %all-reduce.7.cloned.1.call-update) | async-done | bytes 262160 | tf_op jit(solution)/shard_map/psum | solution.py:12
  445.5 99.1 %all-reduce.9.cloned.1.call-done = f32[256,256]{1,0:T(8,128)} async-done(((f32[256,256]{1,0:T(8,128)}), f32[256,256]{1,0:T(8,128)}) %all-reduce.9.cloned.1.call-update) | async-done | bytes 262160 | tf_op jit(solution)/shard_map/psum | solution.py:13
  558.1 1.7 fusion.216
  559.8 1.8 copy.230
  564.3 2.9 fusion.79
  569.6 2.1 fusion.220
  573.7 292.5 %psum.67 = f32[256]{0:T(256)S(1)} all-reduce(f32[256]{0:T(256)S(1)} %get-tuple-element.62), channel_id=1, replica_groups=mesh['dp'=2,'row'=16,'col'=8] {'row','col'}, use_global_device_ids=true, to_apply=%region_7.8 | all-reduce | flops 256 | bytes 2048 | tf_op jit(solution)/shard_map/psum | solution.py:126
  866.3 2.2 convolution_bitcast_fusion.1
  868.6 2.4 fusion.11
  871.0 2.2 copy.273
  873.1 128.3 %all-reduce = (f32[256]{0:T(256)S(1)}, f32[256]{0:T(256)S(1)}) all-reduce(f32[256]{0:T(256)} %get-tuple-element.36, f32[256]{0:T(256)S(1)} %get-tuple-element.35), channel_id=1, replica_groups=mesh['dp'=2,'row'=16,'col'=8] {'dp','row','col'}, use_global_device_ids=true, to_apply=%region_12.13 | all-reduce | flops 512 | bytes 4096 | tf_op jit(solution)/shard_map/psum | solution.py:144
  1003.2 2.2 fusion.90
  1023.0 1.9 multiply_reduce_fusion.1
  1025.8 1.9 fusion.8
  1031.7 3.2 collective-permute-start.4
  1036.8 3.6 collective-permute-done.5
  1041.0 3.7 collective-permute-start.6
  1047.7 2.9 copy.272
  1064.1 241.8 %all-reduce.13.cloned.1.call-done = (f32[256,256]{0,1:T(8,128)}, f32[256,72]{1,0:T(8,128)}) async-done(((f32[256,256]{0,1:T(8,128)}, f32[256,72]{1,0:T(8,128)}), (f32[256,256]{0,1:T(8,128)}, f32[256,72]{1,0:T(8,128)})) %all-reduce.13.cloned.1.call-update) | async-done | bytes 335888 | tf_op jit(solution)/shard_map/psum | solution.py:144
  (300 shorter events, 80.4 us)
Async XLA Ops:
  7.2 562.4 %copy-start = (bf16[256,256]{1,0:T(8,128)(2,1)S(1)}, bf16[256,256]{1,0:T(8,128)(2,1)}, u32[]{:S(2)}) copy-start(bf16[256,256]{1,0:T(8,128)(2,1)} %param.10) | copy-start | bytes 393220
  7.2 6.4 copy-start.73
  7.2 437.6 %all-reduce.7.cloned.1.call-start = ((), (), s32[]{:S(2)}) async-start(), calls=%async_computation | async-start | bytes 524288 | tf_op jit(solution)/shard_map/psum | solution.py:12
  8.4 6.0 collective-permute-start
  12.3 5.0 collective-permute-start.1
  18.1 6.7 collective-permute-start.2
  22.0 4.6 collective-permute-start.3
  24.1 6.4 copy-start.57
  24.3 6.6 copy-start.55
  24.4 6.7 copy-start.53
  24.6 6.9 copy-start.51
  24.8 7.0 copy-start.49
  32.2 297.2 %copy-start.13 = (bf16[1,256,8,128]{3,2,1,0:T(8,128)(2,1)S(1)}, bf16[1,256,8,128]{3,2,1,0:T(8,128)(2,1)}, u32[]{:S(2)}) copy-start(bf16[1,256,8,128]{3,2,1,0:T(8,128)(2,1)} %param.6) | copy-start | bytes 1572868
  329.1 215.5 %all-reduce.9.cloned.1.call-start = ((), (), s32[]{:S(2)}) async-start(), calls=%async_computation.1 | async-start | bytes 524288 | tf_op jit(solution)/shard_map/psum | solution.py:13
  331.3 216.8 %copy-start.45 = (f32[256,256]{1,0:T(8,128)}, f32[256,256]{1,0:T(8,128)S(1)}, u32[]{:S(2)}) copy-start(f32[256,256]{1,0:T(8,128)S(1)} %fusion.88) | copy-start | bytes 786436
  444.8 558.4 %all-reduce.11.cloned.1.call-start = ((), (), s32[]{:S(2)}) async-start(), calls=%async_computation.2 | async-start | bytes 524288 | tf_op jit(solution)/shard_map/psum | solution.py:126
  573.6 295.0 %copy-start.14 = (bf16[256,1024]{1,0:T(8,128)(2,1)S(1)}, bf16[256,1024]{1,0:T(8,128)(2,1)}, u32[]{:S(2)}) copy-start(bf16[256,1024]{1,0:T(8,128)(2,1)} %get-tuple-element.61) | copy-start | bytes 1572868
  573.6 732.3 %all-reduce.13.cloned.1.call-start = ((), (), s32[]{:S(2)}) async-start(), calls=%async_computation.3 | async-start | bytes 786432 | tf_op jit(solution)/shard_map/psum | solution.py:144
  871.0 131.1 %copy-start.34 = (bf16[256,1024]{1,0:T(8,128)(2,1)S(1)}, bf16[256,1024]{1,0:T(8,128)(2,1)}, u32[]{:S(2)}) copy-start(bf16[256,1024]{1,0:T(8,128)(2,1)} %copy-done.33) | copy-start | bytes 1572868
  1031.7 4.9 collective-permute-start.4
  1035.3 5.0 collective-permute-start.5
  1041.0 11.3 collective-permute-start.6
  1045.1 7.7 collective-permute-start.7
  1062.4 247.0 %copy-start.1 = (bf16[256,256]{1,0:T(8,128)(2,1)S(1)}, bf16[256,256]{1,0:T(8,128)(2,1)}, u32[]{:S(2)}) copy-start(bf16[256,256]{1,0:T(8,128)(2,1)} %param.10) | copy-start | bytes 393220
  (64 other events, 129.8 us)
Sparse Core Ops, SparseCore 0:
  329.3 115.5 all-reduce.6
  448.0 96.5 all-reduce.8
  573.8 212.6 all-reduce.10
  1052.5 253.4 all-reduce.12
